TPU v7x, 32 devices: a whole 2x2x4 slice. The times are simulated.
32 devices in a mesh: wide: 16 (over z, x, core), narrow: 2 (over y).
Axes of the slice: x: 2, y: 2, z: 4, core: 2. Of those that a mesh axis runs over, the one named last changes fastest.
Arguments:
- tokens: bfloat16 [2, 32, 320, 1024], P(None, ('wide', 'narrow')), may hold values from -6 to 6
- cotangent: bfloat16 [2, 32, 320, 1024], P(None, ('wide', 'narrow')), may hold values from -6 to 6
- cond: bfloat16 [8, 1024], replicated, may hold values from -6 to 6
- clip_frames: int32 [8], replicated, may hold values from 2 to 9, as said below
- window_clip: int32 [2, 32], P(None, ('wide', 'narrow')), may hold values from 0 to 7
- window_half: int32 [2, 32], P(None, ('wide', 'narrow')), may hold values from 0 to 1
- ada_weight: bfloat16 [1024, 6144], P('narrow', 'wide'), may hold values from -0.1875 to 0.1875
- qkv_weight: bfloat16 [1024, 3072], P('narrow', 'wide'), may hold values from -0.1875 to 0.1875
- out_weight: bfloat16 [1024, 1024], P('narrow', 'wide'), may hold values from -1 to 1
- up_weight: bfloat16 [1024, 4096], P('narrow', 'wide'), may hold values from -0.1875 to 0.1875
- down_weight: bfloat16 [4096, 1024], P('narrow', 'wide'), may hold values from -0.09375 to 0.09375
- offset_table: bfloat16 [16, 39], replicated, may hold values from -3 to 3
Outputs:
- mixed: bfloat16 [2, 32, 320, 1024], P(None, ('wide', 'narrow'))
- grad_tokens: float32 [2, 32, 320, 1024], P(None, ('wide', 'narrow'))
- grad_ada: float32 [1024, 6144], P('narrow', 'wide')
- grad_qkv: float32 [1024, 3072], P('narrow', 'wide')
- grad_out: float32 [1024, 1024], P('narrow', 'wide')
- grad_up: float32 [1024, 4096], P('narrow', 'wide')
- grad_down: float32 [4096, 1024], P('narrow', 'wide')
- grad_table: float32 [16, 39], replicated
Inputs may be any that keep to these rules, and one draw needn't show every extreme that they name: `clip_frames`: latent frames of each clip; short clips are the most common, each longer count about half as frequent as the one below it, and some clip has the most. `window_clip`: a clip number.
All inputs are finite; a program needn't handle non-finite values.
Results may differ from a plain program's by a relative error of at most 0.017.
Values may be sent and summed in bfloat16 or wider, within the bound.
A program may use at most 256 MiB of HBM per device.

v0:
```python
import math
import jax
import jax.numpy as jnp
from jax import lax
from jax.sharding import PartitionSpec as P

HEADS = 16
WIN_FRAMES = 5
WIN_SIDE = 8
epsilon = 1e-06
masked_score = -1e30
highest = lax.Precision.HIGHEST
inv_root_two = 0.7071067811865476
inv_root_tau = 0.3989422804014327


def normalize(values):
    centre = jnp.mean(values, -1, keepdims=True)
    shifted = values - centre
    inv_std = lax.rsqrt(jnp.mean(shifted * shifted, -1, keepdims=True) + epsilon)
    return (shifted * inv_std, inv_std)


def normalize_back(grad_norm, normed, inv_std):
    return inv_std * (
        grad_norm
        - jnp.mean(grad_norm, -1, keepdims=True)
        - normed * jnp.mean(grad_norm * normed, -1, keepdims=True)
    )


def offset_maps():
    frame_pos = jnp.arange(WIN_FRAMES)
    side_pos = jnp.arange(WIN_SIDE)
    frame_off = frame_pos[:, None] - frame_pos[None, :] + WIN_FRAMES - 1
    side_off = side_pos[:, None] - side_pos[None, :] + WIN_SIDE - 1
    frame_map = (frame_off[:, :, None] == jnp.arange(2 * WIN_FRAMES - 1)[None, None, :]).astype(
        jnp.float32
    )
    side_map = (side_off[:, :, None] == jnp.arange(2 * WIN_SIDE - 1)[None, None, :]).astype(
        jnp.float32
    )
    return (frame_map, side_map)


def build_bias(table):
    frame_map, side_map = offset_maps()
    frame_span = 2 * WIN_FRAMES - 1
    side_span = 2 * WIN_SIDE - 1
    along_frame = jnp.einsum("hk,ijk->hij", table[:, :frame_span], frame_map, precision=highest)
    along_row = jnp.einsum(
        "hk,ijk->hij", table[:, frame_span : frame_span + side_span], side_map, precision=highest
    )
    along_col = jnp.einsum(
        "hk,ijk->hij", table[:, frame_span + side_span :], side_map, precision=highest
    )
    full_grid = (
        along_frame[:, :, None, None, :, None, None]
        + along_row[:, None, :, None, None, :, None]
        + along_col[:, None, None, :, None, None, :]
    )
    win_tokens = WIN_FRAMES * WIN_SIDE * WIN_SIDE
    return full_grid.reshape(table.shape[0], win_tokens, win_tokens)


def table_grad(grad_bias):
    frame_map, side_map = offset_maps()
    grid_vals = grad_bias.reshape(
        grad_bias.shape[0], WIN_FRAMES, WIN_SIDE, WIN_SIDE, WIN_FRAMES, WIN_SIDE, WIN_SIDE
    )
    by_frame = jnp.sum(grid_vals, axis=(2, 3, 5, 6))
    by_row = jnp.sum(grid_vals, axis=(1, 3, 4, 6))
    by_col = jnp.sum(grid_vals, axis=(1, 2, 4, 5))
    return jnp.concatenate(
        [
            jnp.einsum("hij,ijk->hk", by_frame, frame_map, precision=highest),
            jnp.einsum("hij,ijk->hk", by_row, side_map, precision=highest),
            jnp.einsum("hij,ijk->hk", by_col, side_map, precision=highest),
        ],
        axis=1,
    )


def live_keys(window_ids, window_halves, clip_frames):
    clip_hits = window_ids[:, None] == jnp.arange(clip_frames.shape[0])[None, :]
    frames_of = jnp.sum(jnp.where(clip_hits, clip_frames[None, :], 0), axis=1)
    live = jnp.clip(frames_of - WIN_FRAMES * window_halves, 1, WIN_FRAMES)
    frame_of_pos = jnp.arange(WIN_FRAMES * WIN_SIDE * WIN_SIDE) // (WIN_SIDE * WIN_SIDE)
    return frame_of_pos[None, :] < live[:, None]


def gelu_slope(pre_act):
    return 0.5 * (1.0 + lax.erf(pre_act * inv_root_two)) + pre_act * inv_root_tau * jnp.exp(
        -0.5 * pre_act * pre_act
    )


def window_scores(queries, keys_in, bias, valid):
    scale_factor = 1.0 / math.sqrt(queries.shape[-1])
    raw_scores = (
        jnp.einsum("wihe,wjhe->whij", queries, keys_in, preferred_element_type=jnp.float32)
        * scale_factor
    )
    return jnp.where(valid[:, None, None, :], raw_scores + bias[None], masked_score)


def gather_weights(ada_part, qkv_part, out_part, up_part, down_part):
    col_full = (
        lax.all_gather(ada_part, "wide", axis=1, tiled=True),
        lax.all_gather(qkv_part, "wide", axis=1, tiled=True),
        lax.all_gather(out_part, "wide", axis=1, tiled=True),
        lax.all_gather(up_part, "wide", axis=1, tiled=True),
        lax.all_gather(down_part, "wide", axis=1, tiled=True),
    )
    return (
        lax.all_gather(col_full[0], "narrow", axis=0, tiled=True),
        lax.all_gather(col_full[1], "narrow", axis=0, tiled=True),
        lax.all_gather(col_full[2], "narrow", axis=0, tiled=True),
        lax.all_gather(col_full[3], "narrow", axis=0, tiled=True),
        lax.all_gather(col_full[4], "narrow", axis=0, tiled=True),
    )


def scatter_grads(grad_set):
    row_owned = (
        lax.psum_scatter(
            grad_set[0].astype(jnp.bfloat16), "narrow", scatter_dimension=0, tiled=True
        ).astype(jnp.float32),
        lax.psum_scatter(
            grad_set[1].astype(jnp.bfloat16), "narrow", scatter_dimension=0, tiled=True
        ).astype(jnp.float32),
        lax.psum_scatter(
            grad_set[2].astype(jnp.bfloat16), "narrow", scatter_dimension=0, tiled=True
        ).astype(jnp.float32),
        lax.psum_scatter(
            grad_set[3].astype(jnp.bfloat16), "narrow", scatter_dimension=0, tiled=True
        ).astype(jnp.float32),
        lax.psum_scatter(
            grad_set[4].astype(jnp.bfloat16), "narrow", scatter_dimension=0, tiled=True
        ).astype(jnp.float32),
    )
    return (
        lax.psum_scatter(
            row_owned[0].astype(jnp.bfloat16), "wide", scatter_dimension=1, tiled=True
        ).astype(jnp.float32),
        lax.psum_scatter(
            row_owned[1].astype(jnp.bfloat16), "wide", scatter_dimension=1, tiled=True
        ).astype(jnp.float32),
        lax.psum_scatter(
            row_owned[2].astype(jnp.bfloat16), "wide", scatter_dimension=1, tiled=True
        ).astype(jnp.float32),
        lax.psum_scatter(
            row_owned[3].astype(jnp.bfloat16), "wide", scatter_dimension=1, tiled=True
        ).astype(jnp.float32),
        lax.psum_scatter(
            row_owned[4].astype(jnp.bfloat16), "wide", scatter_dimension=1, tiled=True
        ).astype(jnp.float32),
    )


def forward_pass(inputs, cond_rows, valid, weights, bias):
    ada_full, qkv_full, out_full, up_full, down_full = weights
    win_count, win_tokens, width = inputs.shape
    cond_act = jax.nn.silu(cond_rows.astype(jnp.float32)).astype(jnp.bfloat16)
    modulation = jnp.dot(cond_act, ada_full, preferred_element_type=jnp.float32).reshape(
        win_count, 6, 1, width
    )
    resid_in = inputs.astype(jnp.float32)
    normed_one, inv_one = normalize(resid_in)
    hidden_one = (normed_one * (1.0 + modulation[:, 1]) + modulation[:, 0]).astype(jnp.bfloat16)
    qkv_vals = jnp.einsum(
        "wtd,de->wte", hidden_one, qkv_full, preferred_element_type=jnp.float32
    ).astype(jnp.bfloat16)
    split_qkv = qkv_vals.reshape(win_count, win_tokens, 3, HEADS, width // HEADS)
    queries = split_qkv[:, :, 0]
    keys_in = split_qkv[:, :, 1]
    values_in = split_qkv[:, :, 2]
    scores = window_scores(queries, keys_in, bias, valid)
    row_peak = jnp.max(scores, -1, keepdims=True)
    exp_scores = jnp.exp(scores - row_peak)
    total_exp = jnp.sum(exp_scores, -1, keepdims=True)
    log_total = row_peak + jnp.log(total_exp)
    probs_low = (exp_scores / total_exp).astype(jnp.bfloat16)
    heads_out = jnp.einsum(
        "whij,wjhe->wihe", probs_low, values_in, preferred_element_type=jnp.float32
    )
    heads_low = heads_out.reshape(win_count, win_tokens, width).astype(jnp.bfloat16)
    attended = jnp.einsum("wtd,de->wte", heads_low, out_full, preferred_element_type=jnp.float32)
    resid_mid = resid_in + modulation[:, 2] * attended
    normed_two, inv_two = normalize(resid_mid)
    hidden_two = (normed_two * (1.0 + modulation[:, 4]) + modulation[:, 3]).astype(jnp.bfloat16)
    up_proj = jnp.einsum("wtd,df->wtf", hidden_two, up_full, preferred_element_type=jnp.float32)
    gelu_low = jax.nn.gelu(up_proj, approximate=False).astype(jnp.bfloat16)
    ffn_out = jnp.einsum("wtf,fd->wtd", gelu_low, down_full, preferred_element_type=jnp.float32)
    result = (resid_mid + modulation[:, 5] * ffn_out).astype(jnp.bfloat16)
    saved_vals = (
        cond_act,
        modulation,
        normed_one,
        inv_one,
        hidden_one,
        queries,
        keys_in,
        values_in,
        log_total,
        heads_low,
        attended,
        normed_two,
        inv_two,
        hidden_two,
        up_proj,
        gelu_low,
        ffn_out,
    )
    return (result, saved_vals)


def backward_pass(grad_out, saved_vals, weights, bias, valid):
    (
        cond_act,
        modulation,
        normed_one,
        inv_one,
        hidden_one,
        queries,
        keys_in,
        values_in,
        log_total,
        heads_low,
        attended,
        normed_two,
        inv_two,
        hidden_two,
        up_proj,
        gelu_low,
        ffn_out,
    ) = saved_vals
    ada_full, qkv_full, out_full, up_full, down_full = weights
    win_count, win_tokens, width = grad_out.shape
    grad_res = grad_out.astype(jnp.float32)
    grad_gate_two = jnp.sum(grad_res * ffn_out, 1)
    grad_ffn = (modulation[:, 5] * grad_res).astype(jnp.bfloat16)
    grad_downw = jnp.einsum("wtf,wtd->fd", gelu_low, grad_ffn, preferred_element_type=jnp.float32)
    grad_gelu = jnp.einsum("wtd,fd->wtf", grad_ffn, down_full, preferred_element_type=jnp.float32)
    grad_pre = (grad_gelu * gelu_slope(up_proj)).astype(jnp.bfloat16)
    grad_upw = jnp.einsum("wtd,wtf->df", hidden_two, grad_pre, preferred_element_type=jnp.float32)
    grad_hidden_two = jnp.einsum(
        "wtf,df->wtd", grad_pre, up_full, preferred_element_type=jnp.float32
    )
    grad_shift_two = jnp.sum(grad_hidden_two, 1)
    grad_scale_two = jnp.sum(grad_hidden_two * normed_two, 1)
    grad_mid = grad_res + normalize_back(
        grad_hidden_two * (1.0 + modulation[:, 4]), normed_two, inv_two
    )
    grad_gate_one = jnp.sum(grad_mid * attended, 1)
    grad_att = (modulation[:, 2] * grad_mid).astype(jnp.bfloat16)
    grad_outw = jnp.einsum("wtd,wte->de", heads_low, grad_att, preferred_element_type=jnp.float32)
    grad_heads = jnp.einsum(
        "wte,de->wtd", grad_att, out_full, preferred_element_type=jnp.float32
    ).astype(jnp.bfloat16)
    grad_heads = grad_heads.reshape(win_count, win_tokens, HEADS, width // HEADS)
    scores = window_scores(queries, keys_in, bias, valid)
    probs = jnp.exp(scores - log_total)
    probs_low = probs.astype(jnp.bfloat16)
    grad_values = jnp.einsum(
        "whij,wihe->wjhe", probs_low, grad_heads, preferred_element_type=jnp.float32
    )
    grad_probs = jnp.einsum(
        "wihe,wjhe->whij", grad_heads, values_in, preferred_element_type=jnp.float32
    )
    grad_scores = probs * (grad_probs - jnp.sum(probs * grad_probs, -1, keepdims=True))
    grad_bias = jnp.sum(grad_scores, 0)
    scores_low = grad_scores.astype(jnp.bfloat16)
    scale_factor = 1.0 / math.sqrt(queries.shape[-1])
    grad_queries = (
        jnp.einsum("whij,wjhe->wihe", scores_low, keys_in, preferred_element_type=jnp.float32)
        * scale_factor
    )
    grad_keys = (
        jnp.einsum("whij,wihe->wjhe", scores_low, queries, preferred_element_type=jnp.float32)
        * scale_factor
    )
    grad_qkv = (
        jnp.stack([grad_queries, grad_keys, grad_values], 2)
        .reshape(win_count, win_tokens, 3 * width)
        .astype(jnp.bfloat16)
    )
    grad_qkvw = jnp.einsum("wtd,wte->de", hidden_one, grad_qkv, preferred_element_type=jnp.float32)
    grad_hidden_one = jnp.einsum(
        "wte,de->wtd", grad_qkv, qkv_full, preferred_element_type=jnp.float32
    )
    grad_shift_one = jnp.sum(grad_hidden_one, 1)
    grad_scale_one = jnp.sum(grad_hidden_one * normed_one, 1)
    grad_input = grad_mid + normalize_back(
        grad_hidden_one * (1.0 + modulation[:, 1]), normed_one, inv_one
    )
    grad_mod = jnp.stack(
        [
            grad_shift_one,
            grad_scale_one,
            grad_gate_one,
            grad_shift_two,
            grad_scale_two,
            grad_gate_two,
        ],
        1,
    )
    grad_mod = grad_mod.reshape(win_count, 6 * width).astype(jnp.bfloat16)
    grad_adaw = jnp.einsum("wc,we->ce", cond_act, grad_mod, preferred_element_type=jnp.float32)
    return (grad_input, (grad_adaw, grad_qkvw, grad_outw, grad_upw, grad_downw), grad_bias)


def body(
    tokens,
    cotangent,
    cond,
    clip_frames,
    window_clip,
    window_half,
    ada_weight,
    qkv_weight,
    out_weight,
    up_weight,
    down_weight,
    offset_table,
):
    table = offset_table.astype(jnp.float32)
    bias = build_bias(table)
    results = []
    input_grads = []
    shard_sums = None
    bias_total = None
    for micro_idx in range(tokens.shape[0]):
        window_ids = window_clip[micro_idx]
        valid = live_keys(window_ids, window_half[micro_idx], clip_frames)
        cond_rows = cond[window_ids]
        fwd_weights = gather_weights(ada_weight, qkv_weight, out_weight, up_weight, down_weight)
        result, saved_vals = forward_pass(tokens[micro_idx], cond_rows, valid, fwd_weights, bias)
        fenced, saved_vals = lax.optimization_barrier(
            ((ada_weight, qkv_weight, out_weight, up_weight, down_weight), saved_vals)
        )
        back_weights = gather_weights(fenced[0], fenced[1], fenced[2], fenced[3], fenced[4])
        grad_input, weight_grads, grad_bias = backward_pass(
            cotangent[micro_idx], saved_vals, back_weights, bias, valid
        )
        results.append(result)
        input_grads.append(grad_input)
        bias_total = grad_bias if micro_idx == 0 else bias_total + grad_bias
        reduced = scatter_grads(weight_grads)
        shard_sums = (
            reduced
            if micro_idx == 0
            else tuple((prior_val + new_val for prior_val, new_val in zip(shard_sums, reduced)))
        )
    grad_table = lax.psum(table_grad(bias_total), ("wide", "narrow"))
    mixed = jnp.stack(results, 0)
    grad_tokens = jnp.stack(input_grads, 0)
    return (
        mixed,
        grad_tokens,
        shard_sums[0],
        shard_sums[1],
        shard_sums[2],
        shard_sums[3],
        shard_sums[4],
        grad_table,
    )


def solution(mesh):
    placed = (
        P(None, ("wide", "narrow"), None, None),
        P(None, ("wide", "narrow"), None, None),
        P(),
        P(),
        P(None, ("wide", "narrow")),
        P(None, ("wide", "narrow")),
        P("narrow", "wide"),
        P("narrow", "wide"),
        P("narrow", "wide"),
        P("narrow", "wide"),
        P("narrow", "wide"),
        P(),
    )
    return jax.shard_map(
        body,
        mesh=mesh,
        in_specs=placed,
        out_specs=(
            P(None, ("wide", "narrow"), None, None),
            P(None, ("wide", "narrow"), None, None),
            P("narrow", "wide"),
            P("narrow", "wide"),
            P("narrow", "wide"),
            P("narrow", "wide"),
            P("narrow", "wide"),
            P(),
        ),
        check_vma=False,
    )
```

profile of v0, /device:TPU:0, one launch (start us, length us, event | category | flops | bytes accessed | tf_op | source)
XLA Modules:
  0.0 3462.1 jit_solution(14667892397251496808)
XLA Ops:
  11.8 63.6 %all-gather.27.cloned.1.call-done = bf16[512,6144]{0,1:T(8,128)(2,1)} async-done(((bf16[512,384]{0,1:T(8,128)(2,1)}), bf16[512,6144]{0,1:T(8,128)(2,1)}) %all-gather.27.cloned.1.call-update) | async-done | bytes 6291472 | tf_op jit(solution)/shard_map/all_gather | solution.py:109
  75.5 46.3 %all-gather.31.cloned.1.call-done = bf16[512,3072]{0,1:T(8,128)(2,1)} async-done(((bf16[512,192]{0,1:T(8,128)(2,1)}), bf16[512,3072]{0,1:T(8,128)(2,1)}) %all-gather.31.cloned.1.call-update) | async-done | bytes 3145744 | tf_op jit(solution)/shard_map/all_gather | solution.py:110
  121.8 38.9 %all-gather.35.cloned.1.call-done = bf16[512,1024]{0,1:T(8,128)(2,1)} async-done(((bf16[512,64]{0,1:T(8,128)(2,1)}), bf16[512,1024]{0,1:T(8,128)(2,1)}) %all-gather.35.cloned.1.call-update) | async-done | bytes 1048592 | tf_op jit(solution)/shard_map/all_gather | solution.py:111
  160.8 54.1 %all-gather.39.cloned.1.call-done = bf16[512,4096]{1,0:T(8,128)(2,1)} async-done(((bf16[512,256]{1,0:T(8,128)(2,1)}), bf16[512,4096]{1,0:T(8,128)(2,1)}) %all-gather.39.cloned.1.call-update) | async-done | bytes 4194320 | tf_op jit(solution)/shard_map/all_gather | solution.py:112
  219.0 17.2 broadcast_add_fusion
  236.3 34.8 %copy.67 = f32[16,320,320]{1,2,0:T(8,128)} copy(f32[16,320,320]{0,2,1:T(8,128)} %bitcast.500) | data formatting | bytes 13107200 | tf_op jit(solution)/shard_map/add | solution.py:58
  279.8 138.5 %all-gather.29.cloned.1.call-done = bf16[1024,6144]{0,1:T(8,128)(2,1)} async-done(((bf16[512,6144]{0,1:T(8,128)(2,1)}), bf16[1024,6144]{0,1:T(8,128)(2,1)}) %all-gather.29.cloned.1.call-update) | async-done | bytes 12582928 | tf_op jit(solution)/shard_map/all_gather | solution.py:116
  430.9 69.4 %all-gather.33.cloned.1.call-done = bf16[1024,3072]{0,1:T(8,128)(2,1)} async-done(((bf16[512,3072]{0,1:T(8,128)(2,1)}), bf16[1024,3072]{0,1:T(8,128)(2,1)}) %all-gather.33.cloned.1.call-update) | async-done | bytes 6291472 | tf_op jit(solution)/shard_map/all_gather | solution.py:117
  555.2 85.4 %all-gather.41.cloned.1.call-done = bf16[1024,4096]{1,0:T(8,128)(2,1)} async-done(((bf16[512,4096]{1,0:T(8,128)(2,1)}), bf16[1024,4096]{1,0:T(8,128)(2,1)}) %all-gather.41.cloned.1.call-update) | async-done | bytes 8388624 | tf_op jit(solution)/shard_map/all_gather | solution.py:119
  640.5 18.6 fusion.11
  659.1 86.8 %all-gather.45.cloned.1.call-done = bf16[4096,1024]{0,1:T(8,128)(2,1)} async-done(((bf16[2048,1024]{0,1:T(8,128)(2,1)}), bf16[4096,1024]{0,1:T(8,128)(2,1)}) %all-gather.45.cloned.1.call-update) | async-done | bytes 8388624 | tf_op jit(solution)/shard_map/all_gather | solution.py:120
  758.5 18.9 fusion.8
  784.8 20.1 all-gather.63.cloned.1.call-done
  804.9 53.7 %all-gather.67.cloned.1.call-done = bf16[512,4096]{1,0:T(8,128)(2,1)} async-done(((bf16[512,256]{1,0:T(8,128)(2,1)}), bf16[512,4096]{1,0:T(8,128)(2,1)}) %all-gather.67.cloned.1.call-update) | async-done | bytes 4194320 | tf_op jit(solution)/shard_map/all_gather | solution.py:112
  858.7 50.9 %all-gather.47.cloned.1.call-done = bf16[2048,1024]{0,1:T(8,128)(2,1)} async-done(((bf16[2048,64]{0,1:T(8,128)(2,1)}), bf16[2048,1024]{0,1:T(8,128)(2,1)}) %all-gather.47.cloned.1.call-update) | async-done | bytes 4194320 | tf_op jit(solution)/shard_map/all_gather | solution.py:113
  909.6 53.7 %all-gather.51.cloned.1.call-done = bf16[512,4096]{1,0:T(8,128)(2,1)} async-done(((bf16[512,256]{1,0:T(8,128)(2,1)}), bf16[512,4096]{1,0:T(8,128)(2,1)}) %all-gather.51.cloned.1.call-update) | async-done | bytes 4194320 | tf_op jit(solution)/shard_map/all_gather | solution.py:112
  963.4 38.1 %all-gather.71.cloned.1.call-done = bf16[512,1024]{0,1:T(8,128)(2,1)} async-done(((bf16[512,64]{0,1:T(8,128)(2,1)}), bf16[512,1024]{0,1:T(8,128)(2,1)}) %all-gather.71.cloned.1.call-update) | async-done | bytes 1048592 | tf_op jit(solution)/shard_map/all_gather | solution.py:111
  1001.6 38.8 %all-gather.55.cloned.1.call-done = bf16[512,1024]{0,1:T(8,128)(2,1)} async-done(((bf16[512,64]{0,1:T(8,128)(2,1)}), bf16[512,1024]{0,1:T(8,128)(2,1)}) %all-gather.55.cloned.1.call-update) | async-done | bytes 1048592 | tf_op jit(solution)/shard_map/all_gather | solution.py:111
  1040.5 46.2 %all-gather.75.cloned.1.call-done = bf16[512,3072]{0,1:T(8,128)(2,1)} async-done(((bf16[512,192]{0,1:T(8,128)(2,1)}), bf16[512,3072]{0,1:T(8,128)(2,1)}) %all-gather.75.cloned.1.call-update) | async-done | bytes 3145744 | tf_op jit(solution)/shard_map/all_gather | solution.py:110
  1086.7 46.3 %all-gather.59.cloned.1.call-done = bf16[512,3072]{0,1:T(8,128)(2,1)} async-done(((bf16[512,192]{0,1:T(8,128)(2,1)}), bf16[512,3072]{0,1:T(8,128)(2,1)}) %all-gather.59.cloned.1.call-update) | async-done | bytes 3145744 | tf_op jit(solution)/shard_map/all_gather | solution.py:110
  1133.2 104.3 %all-gather.65.cloned.1.call-done = bf16[4096,1024]{0,1:T(8,128)(2,1)} async-done(((bf16[2048,1024]{0,1:T(8,128)(2,1)}), bf16[4096,1024]{0,1:T(8,128)(2,1)}) %all-gather.65.cloned.1.call-update) | async-done | bytes 8388624 | tf_op jit(solution)/shard_map/all_gather | solution.py:120
  1246.1 96.8 %all-gather.69.cloned.1.call-done = bf16[1024,4096]{1,0:T(8,128)(2,1)} async-done(((bf16[512,4096]{1,0:T(8,128)(2,1)}), bf16[1024,4096]{1,0:T(8,128)(2,1)}) %all-gather.69.cloned.1.call-update) | async-done | bytes 8388624 | tf_op jit(solution)/shard_map/all_gather | solution.py:119
  1353.8 94.8 %all-gather.49.cloned.1.call-done = bf16[4096,1024]{0,1:T(8,128)(2,1)} async-done(((bf16[2048,1024]{0,1:T(8,128)(2,1)}), bf16[4096,1024]{0,1:T(8,128)(2,1)}) %all-gather.49.cloned.1.call-update) | async-done | bytes 8388624 | tf_op jit(solution)/shard_map/all_gather | solution.py:120
  1456.9 97.2 %all-gather.53.cloned.1.call-done = bf16[1024,4096]{1,0:T(8,128)(2,1)} async-done(((bf16[512,4096]{1,0:T(8,128)(2,1)}), bf16[1024,4096]{1,0:T(8,128)(2,1)}) %all-gather.53.cloned.1.call-update) | async-done | bytes 8388624 | tf_op jit(solution)/shard_map/all_gather | solution.py:119
  1593.5 29.8 all-gather.57.cloned.1.call-done
  1649.3 17.6 fusion.40
  1736.1 51.0 %all-gather.61.cloned.1.call-done = bf16[1024,3072]{0,1:T(8,128)(2,1)} async-done(((bf16[512,3072]{0,1:T(8,128)(2,1)}), bf16[1024,3072]{0,1:T(8,128)(2,1)}) %all-gather.61.cloned.1.call-update) | async-done | bytes 6291472 | tf_op jit(solution)/shard_map/all_gather | solution.py:117
  1801.7 19.5 reduce-scatter.47.cloned.1.call-done
  1823.5 31.8 reduce-scatter.45.cloned.1.call-done
  1857.6 99.3 %reduce-scatter.59.cloned.1.call-done = bf16[2048,1024]{1,0:T(8,128)(2,1)} async-done(((bf16[4096,1024]{1,0:T(8,128)(2,1)}), bf16[2048,1024]{1,0:T(8,128)(2,1)}) %reduce-scatter.59.cloned.1.call-update) | async-done | bytes 4194320 | tf_op jit(solution)/shard_map/reduce_scatter | solution.py:138
  1963.5 94.9 %reduce-scatter.57.cloned.1.call-done = bf16[2048,1024]{1,0:T(8,128)(2,1)} async-done(((bf16[4096,1024]{1,0:T(8,128)(2,1)}), bf16[2048,1024]{1,0:T(8,128)(2,1)}) %reduce-scatter.57.cloned.1.call-update) | async-done | bytes 4194320 | tf_op jit(solution)/shard_map/reduce_scatter | solution.py:138
  2065.0 72.8 %reduce-scatter.43.cloned.1.call-done = bf16[512,3072]{1,0:T(8,128)(2,1)} async-done(((bf16[1024,3072]{1,0:T(8,128)(2,1)}), bf16[512,3072]{1,0:T(8,128)(2,1)}) %reduce-scatter.43.cloned.1.call-update) | async-done | bytes 3145744 | tf_op jit(solution)/shard_map/reduce_scatter | solution.py:129
  2142.5 74.8 %reduce-scatter.41.cloned.1.call-done = bf16[512,3072]{1,0:T(8,128)(2,1)} async-done(((bf16[1024,3072]{1,0:T(8,128)(2,1)}), bf16[512,3072]{1,0:T(8,128)(2,1)}) %reduce-scatter.41.cloned.1.call-update) | async-done | bytes 3145744 | tf_op jit(solution)/shard_map/reduce_scatter | solution.py:129
  2222.0 96.7 %reduce-scatter.53.cloned.1.call-done = bf16[512,4096]{1,0:T(8,128)(2,1)} async-done(((bf16[1024,4096]{1,0:T(8,128)(2,1)}), bf16[512,4096]{1,0:T(8,128)(2,1)}) %reduce-scatter.53.cloned.1.call-update) | async-done | bytes 4194320 | tf_op jit(solution)/shard_map/reduce_scatter | solution.py:135
  2318.8 101.6 %reduce-scatter.49.cloned.1.call-done = bf16[512,4096]{1,0:T(8,128)(2,1)} async-done(((bf16[1024,4096]{1,0:T(8,128)(2,1)}), bf16[512,4096]{1,0:T(8,128)(2,1)}) %reduce-scatter.49.cloned.1.call-update) | async-done | bytes 4194320 | tf_op jit(solution)/shard_map/reduce_scatter | solution.py:135
  2420.7 146.5 %reduce-scatter.39.cloned.1.call-done = bf16[512,6144]{1,0:T(8,128)(2,1)} async-done(((bf16[1024,6144]{1,0:T(8,128)(2,1)}), bf16[512,6144]{1,0:T(8,128)(2,1)}) %reduce-scatter.39.cloned.1.call-update) | async-done | bytes 6291472 | tf_op jit(solution)/shard_map/reduce_scatter | solution.py:126
  2575.9 137.9 %reduce-scatter.37.cloned.1.call-done = bf16[512,6144]{1,0:T(8,128)(2,1)} async-done(((bf16[1024,6144]{1,0:T(8,128)(2,1)}), bf16[512,6144]{1,0:T(8,128)(2,1)}) %reduce-scatter.37.cloned.1.call-update) | async-done | bytes 6291472 | tf_op jit(solution)/shard_map/reduce_scatter | solution.py:126
  2725.0 32.1 copy.82
  2757.1 17.0 fusion.194
  2774.8 39.4 %psum.7 = f32[16,39]{1,0:T(8,128)} all-reduce(f32[16,39]{1,0:T(8,128)S(1)} %pad_maximum_fusion.2), channel_id=1, replica_groups=mesh['wide'=16,'narrow'=2] {'wide','narrow'}, use_global_device_ids=true, to_apply=%region_59.60 | all-reduce | flops 624 | bytes 4992 | tf_op jit(solution)/shard_map/psum | solution.py:355
  2837.1 73.7 %reduce-scatter.75.cloned.1.call-done = bf16[64,2048]{1,0:T(8,128)(2,1)} async-done(((bf16[1024,2048]{1,0:T(8,128)(2,1)}), bf16[64,2048]{1,0:T(8,128)(2,1)}) %reduce-scatter.75.cloned.1.call-update) | async-done | bytes 262160
  2912.0 74.7 %reduce-scatter.73.cloned.1.call-done = bf16[64,2048]{1,0:T(8,128)(2,1)} async-done(((bf16[1024,2048]{1,0:T(8,128)(2,1)}), bf16[64,2048]{1,0:T(8,128)(2,1)}) %reduce-scatter.73.cloned.1.call-update) | async-done | bytes 262160
  2989.2 66.6 %reduce-scatter.67.cloned.1.call-done = bf16[192,512]{1,0:T(8,128)(2,1)} async-done(((bf16[3072,512]{1,0:T(8,128)(2,1)}), bf16[192,512]{1,0:T(8,128)(2,1)}) %reduce-scatter.67.cloned.1.call-update) | async-done | bytes 196624
  3056.8 68.1 %reduce-scatter.65.cloned.1.call-done = bf16[192,512]{1,0:T(8,128)(2,1)} async-done(((bf16[3072,512]{1,0:T(8,128)(2,1)}), bf16[192,512]{1,0:T(8,128)(2,1)}) %reduce-scatter.65.cloned.1.call-update) | async-done | bytes 196624
  3126.9 73.4 %reduce-scatter.55.cloned.1.call-done = bf16[512,256]{1,0:T(8,128)(2,1)} async-done(((bf16[512,4096]{1,0:T(8,128)(2,1)}), bf16[512,256]{1,0:T(8,128)(2,1)}) %reduce-scatter.55.cloned.1.call-update) | async-done | bytes 262160 | tf_op jit(solution)/shard_map/reduce_scatter | solution.py:152
  3200.3 75.9 %reduce-scatter.51.cloned.1.call-done = bf16[512,256]{1,0:T(8,128)(2,1)} async-done(((bf16[512,4096]{1,0:T(8,128)(2,1)}), bf16[512,256]{1,0:T(8,128)(2,1)}) %reduce-scatter.51.cloned.1.call-update) | async-done | bytes 262160 | tf_op jit(solution)/shard_map/reduce_scatter | solution.py:152
  3278.0 86.3 %reduce-scatter.63.cloned.1.call-done = bf16[384,512]{1,0:T(8,128)(2,1)} async-done(((bf16[6144,512]{1,0:T(8,128)(2,1)}), bf16[384,512]{1,0:T(8,128)(2,1)}) %reduce-scatter.63.cloned.1.call-update) | async-done | bytes 393232
  3365.5 87.6 %reduce-scatter.61.cloned.1.call-done = bf16[384,512]{1,0:T(8,128)(2,1)} async-done(((bf16[6144,512]{1,0:T(8,128)(2,1)}), bf16[384,512]{1,0:T(8,128)(2,1)}) %reduce-scatter.61.cloned.1.call-update) | async-done | bytes 393232
  (428 shorter events, 357.6 us)
Async XLA Ops:
  7.2 68.3 %all-gather.27.cloned.1.call-start = ((), (), s32[]{:S(2)}) async-start(), calls=%async_computation.20 | async-start | bytes 6684672 | tf_op jit(solution)/shard_map/all_gather | solution.py:109
  9.2 112.6 %all-gather.31.cloned.1.call-start = ((), (), s32[]{:S(2)}) async-start(), calls=%async_computation.22 | async-start | bytes 3342336 | tf_op jit(solution)/shard_map/all_gather | solution.py:110
  9.9 150.8 %all-gather.35.cloned.1.call-start = ((), (), s32[]{:S(2)}) async-start(), calls=%async_computation.24 | async-start | bytes 1114112 | tf_op jit(solution)/shard_map/all_gather | solution.py:111
  10.6 204.3 %all-gather.39.cloned.1.call-start = ((), (), s32[]{:S(2)}) async-start(), calls=%async_computation.26 | async-start | bytes 4456448 | tf_op jit(solution)/shard_map/all_gather | solution.py:112
  11.2 268.0 %all-gather.43.cloned.1.call-start = ((), (), s32[]{:S(2)}) async-start(), calls=%async_computation.28 | async-start | bytes 4456448 | tf_op jit(solution)/shard_map/all_gather | solution.py:113
  11.8 406.5 %all-gather.29.cloned.1.call-start = ((), (), s32[]{:S(2)}) async-start(), calls=%async_computation.21 | async-start | bytes 18874368 | tf_op jit(solution)/shard_map/all_gather | solution.py:116
  75.5 424.8 %all-gather.33.cloned.1.call-start = ((), (), s32[]{:S(2)}) async-start(), calls=%async_computation.23 | async-start | bytes 9437184 | tf_op jit(solution)/shard_map/all_gather | solution.py:117
  121.8 413.2 %all-gather.37.cloned.1.call-start = ((), (), s32[]{:S(2)}) async-start(), calls=%async_computation.25 | async-start | bytes 3145728 | tf_op jit(solution)/shard_map/all_gather | solution.py:118
  160.7 479.8 %all-gather.41.cloned.1.call-start = ((), (), s32[]{:S(2)}) async-start(), calls=%async_computation.27 | async-start | bytes 12582912 | tf_op jit(solution)/shard_map/all_gather | solution.py:119
  214.9 531.1 %all-gather.45.cloned.1.call-start = ((), (), s32[]{:S(2)}) async-start(), calls=%async_computation.29 | async-start | bytes 12582912 | tf_op jit(solution)/shard_map/all_gather | solution.py:120
  279.1 258.7 %copy-start.70 = (pred[320]{0:T(512)(128)(4,1)}, pred[320]{0:T(512)(128)(4,1)S(1)}, u32[]{:S(2)}) copy-start(pred[320]{0:T(512)(128)(4,1)S(1)} %fusion.186) | copy-start | bytes 964
  279.2 525.7 %all-gather.63.cloned.1.call-start = ((), (), s32[]{:S(2)}) async-start(), calls=%async_computation.38 | async-start | bytes 4456448 | tf_op jit(solution)/shard_map/all_gather | solution.py:113
  754.2 104.5 %all-gather.67.cloned.1.call-start = ((), (), s32[]{:S(2)}) async-start(), calls=%async_computation.40 | async-start | bytes 4456448 | tf_op jit(solution)/shard_map/all_gather | solution.py:112
  754.7 154.8 %all-gather.47.cloned.1.call-start = ((), (), s32[]{:S(2)}) async-start(), calls=%async_computation.30 | async-start | bytes 4456448 | tf_op jit(solution)/shard_map/all_gather | solution.py:113
  781.8 772.2 %copy-start.35 = (f32[1,320,1024]{2,1,0:T(8,128)}, f32[1,320,1024]{2,1,0:T(8,128)S(1)}, u32[]{:S(2)}) copy-start(f32[1,320,1024]{2,1,0:T(8,128)S(1)} %get-tuple-element.55) | copy-start | bytes 3932164
  781.9 181.5 %all-gather.51.cloned.1.call-start = ((), (), s32[]{:S(2)}) async-start(), calls=%async_computation.32 | async-start | bytes 4456448 | tf_op jit(solution)/shard_map/all_gather | solution.py:112
  782.4 219.0 %all-gather.71.cloned.1.call-start = ((), (), s32[]{:S(2)}) async-start(), calls=%async_computation.42 | async-start | bytes 1114112 | tf_op jit(solution)/shard_map/all_gather | solution.py:111
  783.0 257.4 %all-gather.55.cloned.1.call-start = ((), (), s32[]{:S(2)}) async-start(), calls=%async_computation.34 | async-start | bytes 1114112 | tf_op jit(solution)/shard_map/all_gather | solution.py:111
  783.6 303.1 %all-gather.75.cloned.1.call-start = ((), (), s32[]{:S(2)}) async-start(), calls=%async_computation.44 | async-start | bytes 3342336 | tf_op jit(solution)/shard_map/all_gather | solution.py:110
  784.2 348.9 %all-gather.59.cloned.1.call-start = ((), (), s32[]{:S(2)}) async-start(), calls=%async_computation.36 | async-start | bytes 3342336 | tf_op jit(solution)/shard_map/all_gather | solution.py:110
  784.8 452.7 %all-gather.65.cloned.1.call-start = ((), (), s32[]{:S(2)}) async-start(), calls=%async_computation.39 | async-start | bytes 12582912 | tf_op jit(solution)/shard_map/all_gather | solution.py:120
  804.9 538.0 %all-gather.69.cloned.1.call-start = ((), (), s32[]{:S(2)}) async-start(), calls=%async_computation.41 | async-start | bytes 12582912 | tf_op jit(solution)/shard_map/all_gather | solution.py:119
  858.7 589.9 %all-gather.49.cloned.1.call-start = ((), (), s32[]{:S(2)}) async-start(), calls=%async_computation.31 | async-start | bytes 12582912 | tf_op jit(solution)/shard_map/all_gather | solution.py:120
  909.6 644.5 %all-gather.53.cloned.1.call-start = ((), (), s32[]{:S(2)}) async-start(), calls=%async_computation.33 | async-start | bytes 12582912 | tf_op jit(solution)/shard_map/all_gather | solution.py:119
  963.3 625.4 %all-gather.73.cloned.1.call-start = ((), (), s32[]{:S(2)}) async-start(), calls=%async_computation.43 | async-start | bytes 3145728 | tf_op jit(solution)/shard_map/all_gather | solution.py:118
  1001.5 621.8 %all-gather.57.cloned.1.call-start = ((), (), s32[]{:S(2)}) async-start(), calls=%async_computation.35 | async-start | bytes 3145728 | tf_op jit(solution)/shard_map/all_gather | solution.py:118
  1040.4 679.0 %all-gather.77.cloned.1.call-start = ((), (), s32[]{:S(2)}) async-start(), calls=%async_computation.45 | async-start | bytes 9437184 | tf_op jit(solution)/shard_map/all_gather | solution.py:117
  1086.7 700.4 %all-gather.61.cloned.1.call-start = ((), (), s32[]{:S(2)}) async-start(), calls=%async_computation.37 | async-start | bytes 9437184 | tf_op jit(solution)/shard_map/all_gather | solution.py:117
  1133.1 688.0 %reduce-scatter.47.cloned.1.call-start = ((), (), s32[]{:S(2)}) async-start(), calls=%async_computation.51 | async-start | bytes 3145728 | tf_op jit(solution)/shard_map/reduce_scatter | solution.py:132
  1353.6 501.6 %reduce-scatter.45.cloned.1.call-start = ((), (), s32[]{:S(2)}) async-start(), calls=%async_computation.50 | async-start | bytes 3145728 | tf_op jit(solution)/shard_map/reduce_scatter | solution.py:132
  1565.4 391.5 %reduce-scatter.59.cloned.1.call-start = ((), (), s32[]{:S(2)}) async-start(), calls=%async_computation.57 | async-start | bytes 12582912 | tf_op jit(solution)/shard_map/reduce_scatter | solution.py:138
  1575.5 482.9 %reduce-scatter.57.cloned.1.call-start = ((), (), s32[]{:S(2)}) async-start(), calls=%async_computation.56 | async-start | bytes 12582912 | tf_op jit(solution)/shard_map/reduce_scatter | solution.py:138
  1585.3 552.5 %reduce-scatter.43.cloned.1.call-start = ((), (), s32[]{:S(2)}) async-start(), calls=%async_computation.49 | async-start | bytes 9437184 | tf_op jit(solution)/shard_map/reduce_scatter | solution.py:129
  1682.3 535.0 %reduce-scatter.41.cloned.1.call-start = ((), (), s32[]{:S(2)}) async-start(), calls=%async_computation.48 | async-start | bytes 9437184 | tf_op jit(solution)/shard_map/reduce_scatter | solution.py:129
  1699.7 619.0 %reduce-scatter.53.cloned.1.call-start = ((), (), s32[]{:S(2)}) async-start(), calls=%async_computation.54 | async-start | bytes 12582912 | tf_op jit(solution)/shard_map/reduce_scatter | solution.py:135
  1709.2 711.2 %reduce-scatter.49.cloned.1.call-start = ((), (), s32[]{:S(2)}) async-start(), calls=%async_computation.52 | async-start | bytes 12582912 | tf_op jit(solution)/shard_map/reduce_scatter | solution.py:135
  1718.8 848.4 %reduce-scatter.39.cloned.1.call-start = ((), (), s32[]{:S(2)}) async-start(), calls=%async_computation.47 | async-start | bytes 18874368 | tf_op jit(solution)/shard_map/reduce_scatter | solution.py:126
  1735.4 978.4 %reduce-scatter.37.cloned.1.call-start = ((), (), s32[]{:S(2)}) async-start(), calls=%async_computation.46 | async-start | bytes 18874368 | tf_op jit(solution)/shard_map/reduce_scatter | solution.py:126
  1801.6 1017.2 %reduce-scatter.71.cloned.1.call-start = ((), (), s32[]{:S(2)}) async-start(), calls=%async_computation.63 | async-start | bytes 1114112
  1823.4 1011.9 %reduce-scatter.69.cloned.1.call-start = ((), (), s32[]{:S(2)}) async-start(), calls=%async_computation.62 | async-start | bytes 1114112
  1857.6 1053.2 %reduce-scatter.75.cloned.1.call-start = ((), (), s32[]{:S(2)}) async-start(), calls=%async_computation.65 | async-start | bytes 4456448
  1963.5 1023.3 %reduce-scatter.73.cloned.1.call-start = ((), (), s32[]{:S(2)}) async-start(), calls=%async_computation.64 | async-start | bytes 4456448
  2065.0 990.8 %reduce-scatter.67.cloned.1.call-start = ((), (), s32[]{:S(2)}) async-start(), calls=%async_computation.61 | async-start | bytes 3342336
  2142.5 982.4 %reduce-scatter.65.cloned.1.call-start = ((), (), s32[]{:S(2)}) async-start(), calls=%async_computation.60 | async-start | bytes 3342336
  2222.0 978.3 %reduce-scatter.55.cloned.1.call-start = ((), (), s32[]{:S(2)}) async-start(), calls=%async_computation.55 | async-start | bytes 4456448 | tf_op jit(solution)/shard_map/reduce_scatter | solution.py:152
  2318.7 957.4 %reduce-scatter.51.cloned.1.call-start = ((), (), s32[]{:S(2)}) async-start(), calls=%async_computation.53 | async-start | bytes 4456448 | tf_op jit(solution)/shard_map/reduce_scatter | solution.py:152
  2420.4 943.9 %reduce-scatter.63.cloned.1.call-start = ((), (), s32[]{:S(2)}) async-start(), calls=%async_computation.59 | async-start | bytes 6684672
  2575.9 877.3 %reduce-scatter.61.cloned.1.call-start = ((), (), s32[]{:S(2)}) async-start(), calls=%async_computation.58 | async-start | bytes 6684672
  (83 other events, 1881.5 us)
Sparse Core Ops, SparseCore 0:
  10.9 64.5 all-gather.26
  77.7 44.0 all-gather.30
  123.9 36.7 all-gather.34
  162.7 52.1 all-gather.38
  216.9 48.8 all-gather.42
  267.2 151.0 all-gather.28
  419.8 80.3 all-gather.32
  501.8 33.1 all-gather.36
  536.5 103.9 all-gather.40
  641.9 104.0 all-gather.44
  754.3 50.5 all-gather.62
  806.9 51.7 all-gather.66
  860.8 48.7 all-gather.46
  911.6 51.7 all-gather.50
  965.3 36.1 all-gather.70
  1003.5 36.8 all-gather.54
  1042.5 44.0 all-gather.74
  1088.8 44.2 all-gather.58
  1134.6 102.8 all-gather.64
  1238.8 103.9 all-gather.68
  1344.4 104.0 all-gather.48
  1450.1 103.9 all-gather.52
  1555.6 33.1 all-gather.72
  1590.2 33.1 all-gather.56
  1624.9 80.3 all-gather.76
  1706.7 80.3 all-gather.60
  1789.2 31.8 reduce-scatter.46
  1823.4 31.8 reduce-scatter.44
  1857.6 99.2 reduce-scatter.58
  1959.1 99.2 reduce-scatter.56
  2060.7 77.0 reduce-scatter.42
  2140.2 77.0 reduce-scatter.40
  2219.4 99.2 reduce-scatter.52
  2321.1 99.2 reduce-scatter.48
  2422.7 144.4 reduce-scatter.38
  2569.3 144.4 reduce-scatter.36
  2717.3 57.4 reduce-scatter.70
  2778.8 56.4 reduce-scatter.68
  2839.0 71.7 reduce-scatter.74
  2915.1 71.5 reduce-scatter.72
  2990.5 65.1 reduce-scatter.66
  3059.6 65.2 reduce-scatter.64
  3128.6 71.6 reduce-scatter.54
  3204.7 71.4 reduce-scatter.50
  3280.0 84.3 reduce-scatter.62
  3368.6 84.4 reduce-scatter.60
where the time goes:
time: 3470 us; the launch traced here: 3460 us
  waiting for transfers between devices  2920 us (84%)
  matrix products  228 us (7%)
  local copies, waits for them, and re-layouts  155 us (4%)
  other arithmetic  93.8 us (3%)
  blocking collectives  39.4 us (1%)
    unnamed x54, waiting for transfers between devices  479 us
    all_gather x3, waiting for transfers between devices, gather_weights(): lax.all_gather(col_full[4], 'narrow', axis=0, tiled=True)  286 us
    reduce_scatter x2, waiting for transfers between devices, scatter_grads(): lax.psum_scatter(grad_set[0].astype(jnp.bfloat16), 'narrow', scatter_dime...  284 us
    all_gather x3, waiting for transfers between devices, gather_weights(): lax.all_gather(col_full[3], 'narrow', axis=0, tiled=True)  279 us
    reduce_scatter x2, waiting for transfers between devices, scatter_grads(): lax.psum_scatter(grad_set[3].astype(jnp.bfloat16), 'narrow', scatter_dime...  198 us
    reduce_scatter x2, waiting for transfers between devices, scatter_grads(): lax.psum_scatter(grad_set[4].astype(jnp.bfloat16), 'narrow', scatter_dime...  194 us
    all_gather x3, waiting for transfers between devices, gather_weights(): lax.all_gather(up_part, 'wide', axis=1, tiled=True)  161 us
    reduce_scatter x2, waiting for transfers between devices, scatter_grads(): lax.psum_scatter(row_owned[3].astype(jnp.bfloat16), 'wide', scatter_dimen...  149 us
  transfers between devices with their start and end apart: 46, of which 43 were waited for; matrix products, arithmetic and copies ran while one was open for 13% of the time, Pallas kernels for 0%

commit v1 on v0

--- a/solution.py
+++ b/solution.py
@@ -12,6 +12,18 @@
 highest = lax.Precision.HIGHEST
 inv_root_two = 0.7071067811865476
 inv_root_tau = 0.3989422804014327
+
+
+def ring_gather(array, axis, dim):
+    ways, here, step = (lax.axis_size(axis), lax.axis_index(axis), array.shape[dim])
+    shape = [n * ways if d == dim else n for d, n in enumerate(array.shape)]
+    full = lax.dynamic_update_slice_in_dim(
+        jnp.zeros(shape, array.dtype), array, here * step, axis=dim
+    )
+    for far in range(1, ways):
+        array = lax.ppermute(array, axis, [(d, (d + 1) % ways) for d in range(ways)])
+        full = lax.dynamic_update_slice_in_dim(full, array, (here - far) % ways * step, axis=dim)
+    return full
 
 
 def normalize(values):
@@ -110,7 +122,7 @@
         lax.all_gather(qkv_part, "wide", axis=1, tiled=True),
         lax.all_gather(out_part, "wide", axis=1, tiled=True),
         lax.all_gather(up_part, "wide", axis=1, tiled=True),
-        lax.all_gather(down_part, "wide", axis=1, tiled=True),
+        ring_gather(down_part, "wide", 1),
     )
     return (
         lax.all_gather(col_full[0], "narrow", axis=0, tiled=True),

time: 3470 us -> 3340 us (0.963)
  waiting for transfers between devices: 2920 us -> 2740 us
  local copies, waits for them, and re-layouts: 155 us -> 197 us
    ppermute x0 -> x45, waiting for transfers between devices: none -> 352 us  [ring_gather(): lax.ppermute(array, axis, [(d, (d + 1) % ways) for d in range(ways)])]
    all_gather x1, waiting for transfers between devices: 139 us -> 0.02 us  [gather_weights(): lax.all_gather(col_full[0], 'narrow', axis=0, tiled=True)]
    all_gather x3, waiting for transfers between devices: 161 us -> 53.6 us  [gather_weights(): lax.all_gather(up_part, 'wide', axis=1, tiled=True)]
    all_gather x3, waiting for transfers between devices: 139 us -> 46.3 us  [gather_weights(): lax.all_gather(qkv_part, 'wide', axis=1, tiled=True)]
    all_gather x3, waiting for transfers between devices: 116 us -> 38.9 us  [gather_weights(): lax.all_gather(out_part, 'wide', axis=1, tiled=True)]
    all_gather x3 -> x0, waiting for transfers between devices: 70.9 us -> none  [gather_weights(): lax.all_gather(down_part, 'wide', axis=1, tiled=True)]
    dynamic_update_slice x0 -> x48, local copies, waits for them, and re-layouts: none -> 35.5 us  [the longest x45 33.4 us: ring_gather(): lax.dynamic_update_slice_in_dim(full, array, (here - far) % ways * step,...]
    unnamed x54 -> x51, waiting for transfers between devices: 479 us -> 481 us
  transfers between devices with their start and end apart: 46 -> 88, of which waited for: 43 -> 76; matrix products, arithmetic and copies ran while one was open for 13% -> 15% of each run, Pallas kernels for 0% -> 0%
where the time goes in v1:
time: 3340 us; the launch traced here: 3330 us
  waiting for transfers between devices  2740 us (82%)
  matrix products  228 us (7%)
  local copies, waits for them, and re-layouts  197 us (6%)
  other arithmetic  97.4 us (3%)
  blocking collectives  39.3 us (1%)
    unnamed x51, waiting for transfers between devices  481 us
    ppermute x45, waiting for transfers between devices, ring_gather(): lax.ppermute(array, axis, [(d, (d + 1) % ways) for d in range(ways)])  352 us
    reduce_scatter x2, waiting for transfers between devices, scatter_grads(): lax.psum_scatter(grad_set[0].astype(jnp.bfloat16), 'narrow', scatter_dime...  284 us
    all_gather x3, waiting for transfers between devices, gather_weights(): lax.all_gather(col_full[3], 'narrow', axis=0, tiled=True)  280 us
    all_gather x3, waiting for transfers between devices, gather_weights(): lax.all_gather(col_full[4], 'narrow', axis=0, tiled=True)  254 us
    reduce_scatter x2, waiting for transfers between devices, scatter_grads(): lax.psum_scatter(grad_set[3].astype(jnp.bfloat16), 'narrow', scatter_dime...  198 us
    reduce_scatter x2, waiting for transfers between devices, scatter_grads(): lax.psum_scatter(grad_set[4].astype(jnp.bfloat16), 'narrow', scatter_dime...  194 us
    reduce_scatter x2, waiting for transfers between devices, scatter_grads(): lax.psum_scatter(row_owned[3].astype(jnp.bfloat16), 'wide', scatter_dimen...  149 us
  transfers between devices with their start and end apart: 88, of which 76 were waited for; matrix products, arithmetic and copies ran while one was open for 15% of the time, Pallas kernels for 0%

profile of v1, /device:TPU:0, one launch (start us, length us, event | category | flops | bytes accessed | tf_op | source)
XLA Modules:
  0.0 3334.2 jit_solution(7626081231357044460)
XLA Ops:
  11.3 64.2 %all-gather.24.cloned.1.call-done = bf16[512,6144]{0,1:T(8,128)(2,1)} async-done(((bf16[512,384]{0,1:T(8,128)(2,1)}), bf16[512,6144]{0,1:T(8,128)(2,1)}) %all-gather.24.cloned.1.call-update) | async-done | bytes 6291472 | tf_op jit(solution)/shard_map/all_gather | solution.py:121
  75.5 46.3 %all-gather.28.cloned.1.call-done = bf16[512,3072]{0,1:T(8,128)(2,1)} async-done(((bf16[512,192]{0,1:T(8,128)(2,1)}), bf16[512,3072]{0,1:T(8,128)(2,1)}) %all-gather.28.cloned.1.call-update) | async-done | bytes 3145744 | tf_op jit(solution)/shard_map/all_gather | solution.py:122
  121.8 38.9 %all-gather.32.cloned.1.call-done = bf16[512,1024]{0,1:T(8,128)(2,1)} async-done(((bf16[512,64]{0,1:T(8,128)(2,1)}), bf16[512,1024]{0,1:T(8,128)(2,1)}) %all-gather.32.cloned.1.call-update) | async-done | bytes 1048592 | tf_op jit(solution)/shard_map/all_gather | solution.py:123
  161.3 53.6 %all-gather.36.cloned.1.call-done = bf16[512,4096]{1,0:T(8,128)(2,1)} async-done(((bf16[512,256]{1,0:T(8,128)(2,1)}), bf16[512,4096]{1,0:T(8,128)(2,1)}) %all-gather.36.cloned.1.call-update) | async-done | bytes 4194320 | tf_op jit(solution)/shard_map/all_gather | solution.py:124
  223.7 20.7 broadcast_add_fusion
  279.1 34.2 %copy.67 = f32[16,320,320]{1,2,0:T(8,128)} copy(f32[16,320,320]{0,2,1:T(8,128)} %bitcast.499) | data formatting | bytes 13107200 | tf_op jit(solution)/shard_map/add | solution.py:70
  391.6 57.3 %all-gather.30.cloned.1.call-done = bf16[1024,3072]{0,1:T(8,128)(2,1)} async-done(((bf16[512,3072]{0,1:T(8,128)(2,1)}), bf16[1024,3072]{0,1:T(8,128)(2,1)}) %all-gather.30.cloned.1.call-update) | async-done | bytes 6291472 | tf_op jit(solution)/shard_map/all_gather | solution.py:129
  503.8 85.3 %all-gather.38.cloned.1.call-done = bf16[1024,4096]{1,0:T(8,128)(2,1)} async-done(((bf16[512,4096]{1,0:T(8,128)(2,1)}), bf16[1024,4096]{1,0:T(8,128)(2,1)}) %all-gather.38.cloned.1.call-update) | async-done | bytes 8388624 | tf_op jit(solution)/shard_map/all_gather | solution.py:131
  589.1 18.8 fusion.11
  607.9 86.8 %all-gather.40.cloned.1.call-done = bf16[4096,1024]{0,1:T(8,128)(2,1)} async-done(((bf16[2048,1024]{0,1:T(8,128)(2,1)}), bf16[4096,1024]{0,1:T(8,128)(2,1)}) %all-gather.40.cloned.1.call-update) | async-done | bytes 8388624 | tf_op jit(solution)/shard_map/all_gather | solution.py:132
  706.7 18.3 fusion.8
  732.1 14.0 collective-permute-done.30
  746.1 13.4 collective-permute-done.31
  768.0 11.3 collective-permute-done.33
  799.7 12.4 collective-permute-done.36
  885.2 11.4 collective-permute-done.15
  913.6 12.5 collective-permute-done.18
  934.7 11.5 collective-permute-done.20
  965.9 11.1 collective-permute-done.23
  1036.9 72.6 %all-gather.56.cloned.1.call-done = bf16[4096,1024]{0,1:T(8,128)(2,1)} async-done(((bf16[2048,1024]{0,1:T(8,128)(2,1)}), bf16[4096,1024]{0,1:T(8,128)(2,1)}) %all-gather.56.cloned.1.call-update) | async-done | bytes 8388624 | tf_op jit(solution)/shard_map/all_gather | solution.py:132
  1118.0 97.0 %all-gather.60.cloned.1.call-done = bf16[1024,4096]{1,0:T(8,128)(2,1)} async-done(((bf16[512,4096]{1,0:T(8,128)(2,1)}), bf16[1024,4096]{1,0:T(8,128)(2,1)}) %all-gather.60.cloned.1.call-update) | async-done | bytes 8388624 | tf_op jit(solution)/shard_map/all_gather | solution.py:131
  1226.2 94.2 %all-gather.42.cloned.1.call-done = bf16[4096,1024]{0,1:T(8,128)(2,1)} async-done(((bf16[2048,1024]{0,1:T(8,128)(2,1)}), bf16[4096,1024]{0,1:T(8,128)(2,1)}) %all-gather.42.cloned.1.call-update) | async-done | bytes 8388624 | tf_op jit(solution)/shard_map/all_gather | solution.py:132
  1328.7 97.3 %all-gather.46.cloned.1.call-done = bf16[1024,4096]{1,0:T(8,128)(2,1)} async-done(((bf16[512,4096]{1,0:T(8,128)(2,1)}), bf16[1024,4096]{1,0:T(8,128)(2,1)}) %all-gather.46.cloned.1.call-update) | async-done | bytes 8388624 | tf_op jit(solution)/shard_map/all_gather | solution.py:131
  1465.3 30.0 all-gather.50.cloned.1.call-done
  1521.1 17.6 fusion.40
  1607.6 51.6 %all-gather.54.cloned.1.call-done = bf16[1024,3072]{0,1:T(8,128)(2,1)} async-done(((bf16[512,3072]{0,1:T(8,128)(2,1)}), bf16[1024,3072]{0,1:T(8,128)(2,1)}) %all-gather.54.cloned.1.call-update) | async-done | bytes 6291472 | tf_op jit(solution)/shard_map/all_gather | solution.py:129
  1673.8 19.3 reduce-scatter.47.cloned.1.call-done
  1695.5 31.8 reduce-scatter.45.cloned.1.call-done
  1729.7 99.1 %reduce-scatter.59.cloned.1.call-done = bf16[2048,1024]{1,0:T(8,128)(2,1)} async-done(((bf16[4096,1024]{1,0:T(8,128)(2,1)}), bf16[2048,1024]{1,0:T(8,128)(2,1)}) %reduce-scatter.59.cloned.1.call-update) | async-done | bytes 4194320 | tf_op jit(solution)/shard_map/reduce_scatter | solution.py:150
  1835.4 94.9 %reduce-scatter.57.cloned.1.call-done = bf16[2048,1024]{1,0:T(8,128)(2,1)} async-done(((bf16[4096,1024]{1,0:T(8,128)(2,1)}), bf16[2048,1024]{1,0:T(8,128)(2,1)}) %reduce-scatter.57.cloned.1.call-update) | async-done | bytes 4194320 | tf_op jit(solution)/shard_map/reduce_scatter | solution.py:150
  1936.9 72.8 %reduce-scatter.43.cloned.1.call-done = bf16[512,3072]{1,0:T(8,128)(2,1)} async-done(((bf16[1024,3072]{1,0:T(8,128)(2,1)}), bf16[512,3072]{1,0:T(8,128)(2,1)}) %reduce-scatter.43.cloned.1.call-update) | async-done | bytes 3145744 | tf_op jit(solution)/shard_map/reduce_scatter | solution.py:141
  2014.4 74.8 %reduce-scatter.41.cloned.1.call-done = bf16[512,3072]{1,0:T(8,128)(2,1)} async-done(((bf16[1024,3072]{1,0:T(8,128)(2,1)}), bf16[512,3072]{1,0:T(8,128)(2,1)}) %reduce-scatter.41.cloned.1.call-update) | async-done | bytes 3145744 | tf_op jit(solution)/shard_map/reduce_scatter | solution.py:141
  2093.9 96.7 %reduce-scatter.53.cloned.1.call-done = bf16[512,4096]{1,0:T(8,128)(2,1)} async-done(((bf16[1024,4096]{1,0:T(8,128)(2,1)}), bf16[512,4096]{1,0:T(8,128)(2,1)}) %reduce-scatter.53.cloned.1.call-update) | async-done | bytes 4194320 | tf_op jit(solution)/shard_map/reduce_scatter | solution.py:147
  2190.7 101.6 %reduce-scatter.49.cloned.1.call-done = bf16[512,4096]{1,0:T(8,128)(2,1)} async-done(((bf16[1024,4096]{1,0:T(8,128)(2,1)}), bf16[512,4096]{1,0:T(8,128)(2,1)}) %reduce-scatter.49.cloned.1.call-update) | async-done | bytes 4194320 | tf_op jit(solution)/shard_map/reduce_scatter | solution.py:147
  2292.5 146.5 %reduce-scatter.39.cloned.1.call-done = bf16[512,6144]{1,0:T(8,128)(2,1)} async-done(((bf16[1024,6144]{1,0:T(8,128)(2,1)}), bf16[512,6144]{1,0:T(8,128)(2,1)}) %reduce-scatter.39.cloned.1.call-update) | async-done | bytes 6291472 | tf_op jit(solution)/shard_map/reduce_scatter | solution.py:138
  2447.8 137.9 %reduce-scatter.37.cloned.1.call-done = bf16[512,6144]{1,0:T(8,128)(2,1)} async-done(((bf16[1024,6144]{1,0:T(8,128)(2,1)}), bf16[512,6144]{1,0:T(8,128)(2,1)}) %reduce-scatter.37.cloned.1.call-update) | async-done | bytes 6291472 | tf_op jit(solution)/shard_map/reduce_scatter | solution.py:138
  2596.9 32.0 copy.82
  2628.9 17.0 fusion.196
  2646.6 39.3 %psum.7 = f32[16,39]{1,0:T(8,128)} all-reduce(f32[16,39]{1,0:T(8,128)S(1)} %pad_maximum_fusion.2), channel_id=1, replica_groups=mesh['wide'=16,'narrow'=2] {'wide','narrow'}, use_global_device_ids=true, to_apply=%region_59.60 | all-reduce | flops 624 | bytes 4992 | tf_op jit(solution)/shard_map/psum | solution.py:367
  2691.5 15.9 reduce-scatter.69.cloned.1.call-done
  2709.2 73.4 %reduce-scatter.75.cloned.1.call-done = bf16[64,2048]{1,0:T(8,128)(2,1)} async-done(((bf16[1024,2048]{1,0:T(8,128)(2,1)}), bf16[64,2048]{1,0:T(8,128)(2,1)}) %reduce-scatter.75.cloned.1.call-update) | async-done | bytes 262160
  2783.9 74.7 %reduce-scatter.73.cloned.1.call-done = bf16[64,2048]{1,0:T(8,128)(2,1)} async-done(((bf16[1024,2048]{1,0:T(8,128)(2,1)}), bf16[64,2048]{1,0:T(8,128)(2,1)}) %reduce-scatter.73.cloned.1.call-update) | async-done | bytes 262160
  2861.1 66.7 %reduce-scatter.67.cloned.1.call-done = bf16[192,512]{1,0:T(8,128)(2,1)} async-done(((bf16[3072,512]{1,0:T(8,128)(2,1)}), bf16[192,512]{1,0:T(8,128)(2,1)}) %reduce-scatter.67.cloned.1.call-update) | async-done | bytes 196624
  2928.8 67.7 %reduce-scatter.65.cloned.1.call-done = bf16[192,512]{1,0:T(8,128)(2,1)} async-done(((bf16[3072,512]{1,0:T(8,128)(2,1)}), bf16[192,512]{1,0:T(8,128)(2,1)}) %reduce-scatter.65.cloned.1.call-update) | async-done | bytes 196624
  2998.5 73.1 %reduce-scatter.55.cloned.1.call-done = bf16[512,256]{1,0:T(8,128)(2,1)} async-done(((bf16[512,4096]{1,0:T(8,128)(2,1)}), bf16[512,256]{1,0:T(8,128)(2,1)}) %reduce-scatter.55.cloned.1.call-update) | async-done | bytes 262160 | tf_op jit(solution)/shard_map/reduce_scatter | solution.py:164
  3071.6 76.1 %reduce-scatter.51.cloned.1.call-done = bf16[512,256]{1,0:T(8,128)(2,1)} async-done(((bf16[512,4096]{1,0:T(8,128)(2,1)}), bf16[512,256]{1,0:T(8,128)(2,1)}) %reduce-scatter.51.cloned.1.call-update) | async-done | bytes 262160 | tf_op jit(solution)/shard_map/reduce_scatter | solution.py:164
  3149.6 86.4 %reduce-scatter.63.cloned.1.call-done = bf16[384,512]{1,0:T(8,128)(2,1)} async-done(((bf16[6144,512]{1,0:T(8,128)(2,1)}), bf16[384,512]{1,0:T(8,128)(2,1)}) %reduce-scatter.63.cloned.1.call-update) | async-done | bytes 393232
  3237.2 87.7 %reduce-scatter.61.cloned.1.call-done = bf16[384,512]{1,0:T(8,128)(2,1)} async-done(((bf16[6144,512]{1,0:T(8,128)(2,1)}), bf16[384,512]{1,0:T(8,128)(2,1)}) %reduce-scatter.61.cloned.1.call-update) | async-done | bytes 393232
  (567 shorter events, 643.1 us)
Async XLA Ops:
  7.2 68.3 %all-gather.24.cloned.1.call-start = ((), (), s32[]{:S(2)}) async-start(), calls=%async_computation.20 | async-start | bytes 6684672 | tf_op jit(solution)/shard_map/all_gather | solution.py:121
  9.2 112.6 %all-gather.28.cloned.1.call-start = ((), (), s32[]{:S(2)}) async-start(), calls=%async_computation.22 | async-start | bytes 3342336 | tf_op jit(solution)/shard_map/all_gather | solution.py:122
  9.9 150.8 %all-gather.32.cloned.1.call-start = ((), (), s32[]{:S(2)}) async-start(), calls=%async_computation.24 | async-start | bytes 1114112 | tf_op jit(solution)/shard_map/all_gather | solution.py:123
  10.6 204.3 %all-gather.36.cloned.1.call-start = ((), (), s32[]{:S(2)}) async-start(), calls=%async_computation.26 | async-start | bytes 4456448 | tf_op jit(solution)/shard_map/all_gather | solution.py:124
  11.2 366.6 %all-gather.26.cloned.1.call-start = ((), (), s32[]{:S(2)}) async-start(), calls=%async_computation.21 | async-start | bytes 18874368 | tf_op jit(solution)/shard_map/all_gather | solution.py:128
  75.5 373.4 %all-gather.30.cloned.1.call-start = ((), (), s32[]{:S(2)}) async-start(), calls=%async_computation.23 | async-start | bytes 9437184 | tf_op jit(solution)/shard_map/all_gather | solution.py:129
  121.8 361.8 %all-gather.34.cloned.1.call-start = ((), (), s32[]{:S(2)}) async-start(), calls=%async_computation.25 | async-start | bytes 3145728 | tf_op jit(solution)/shard_map/all_gather | solution.py:130
  160.7 428.4 %all-gather.38.cloned.1.call-start = ((), (), s32[]{:S(2)}) async-start(), calls=%async_computation.27 | async-start | bytes 12582912 | tf_op jit(solution)/shard_map/all_gather | solution.py:131
  160.8 54.4 %collective-permute-start = (bf16[2048,64]{0,1:T(8,128)(2,1)S(1)}, bf16[2048,64]{0,1:T(8,128)(2,1)S(1)}, u32[]{:S(2)}, u32[]{:S(2)}) collective-permute-start(bf16[2048,64]{0,1:T(8,128)(2,1)S(1)} %copy-done.49), channel_id=1, source_target_pairs={{0,2},{2,4},{4,6},{6,8},{8,10},{10,12},{12,14},{14,16},{16,18},{18... | collective-permute-start | bytes 786440 | tf_op jit(solution)/shard_map/ppermute | solution.py:24
  214.9 479.8 %all-gather.40.cloned.1.call-start = ((), (), s32[]{:S(2)}) async-start(), calls=%async_computation.28 | async-start | bytes 12582912 | tf_op jit(solution)/shard_map/all_gather | solution.py:132
  223.7 21.0 collective-permute-start.2
  278.7 38.4 %collective-permute-start.7 = (bf16[2048,64]{0,1:T(8,128)(2,1)S(1)}, bf16[2048,64]{0,1:T(8,128)(2,1)}, u32[]{:S(2)}, u32[]{:S(2)}) collective-permute-start(bf16[2048,64]{0,1:T(8,128)(2,1)S(1)} %collective-permute-done.6), channel_id=1, source_target_pairs={{0,2},{2,4},{4,6},{6,8},{8,10},{10,12},{12,14},{14,16},{16,18},{18... | collective-permute-start | bytes 786440 | tf_op jit(solution)/shard_map/ppermute | solution.py:24
  377.5 507.1 %all-gather.58.cloned.1.call-start = ((), (), s32[]{:S(2)}) async-start(), calls=%async_computation.37 | async-start | bytes 4456448 | tf_op jit(solution)/shard_map/all_gather | solution.py:124
  702.9 330.4 %all-gather.44.cloned.1.call-start = ((), (), s32[]{:S(2)}) async-start(), calls=%async_computation.30 | async-start | bytes 4456448 | tf_op jit(solution)/shard_map/all_gather | solution.py:124
  729.5 304.6 %all-gather.62.cloned.1.call-start = ((), (), s32[]{:S(2)}) async-start(), calls=%async_computation.39 | async-start | bytes 1114112 | tf_op jit(solution)/shard_map/all_gather | solution.py:123
  730.1 304.6 %all-gather.48.cloned.1.call-start = ((), (), s32[]{:S(2)}) async-start(), calls=%async_computation.32 | async-start | bytes 1114112 | tf_op jit(solution)/shard_map/all_gather | solution.py:123
  730.9 304.5 %all-gather.66.cloned.1.call-start = ((), (), s32[]{:S(2)}) async-start(), calls=%async_computation.41 | async-start | bytes 3342336 | tf_op jit(solution)/shard_map/all_gather | solution.py:122
  731.4 304.7 %all-gather.52.cloned.1.call-start = ((), (), s32[]{:S(2)}) async-start(), calls=%async_computation.34 | async-start | bytes 3342336 | tf_op jit(solution)/shard_map/all_gather | solution.py:122
  732.0 377.5 %all-gather.56.cloned.1.call-start = ((), (), s32[]{:S(2)}) async-start(), calls=%async_computation.36 | async-start | bytes 12582912 | tf_op jit(solution)/shard_map/all_gather | solution.py:132
  732.1 14.0 collective-permute-start.30
  746.1 13.4 collective-permute-start.31
  884.5 330.5 %all-gather.60.cloned.1.call-start = ((), (), s32[]{:S(2)}) async-start(), calls=%async_computation.38 | async-start | bytes 12582912 | tf_op jit(solution)/shard_map/all_gather | solution.py:131
  885.1 435.3 %all-gather.42.cloned.1.call-start = ((), (), s32[]{:S(2)}) async-start(), calls=%async_computation.29 | async-start | bytes 12582912 | tf_op jit(solution)/shard_map/all_gather | solution.py:132
  1033.3 392.7 %all-gather.46.cloned.1.call-start = ((), (), s32[]{:S(2)}) async-start(), calls=%async_computation.31 | async-start | bytes 12582912 | tf_op jit(solution)/shard_map/all_gather | solution.py:131
  1034.0 426.5 %all-gather.64.cloned.1.call-start = ((), (), s32[]{:S(2)}) async-start(), calls=%async_computation.40 | async-start | bytes 3145728 | tf_op jit(solution)/shard_map/all_gather | solution.py:130
  1034.6 460.7 %all-gather.50.cloned.1.call-start = ((), (), s32[]{:S(2)}) async-start(), calls=%async_computation.33 | async-start | bytes 3145728 | tf_op jit(solution)/shard_map/all_gather | solution.py:130
  1035.3 555.5 %all-gather.68.cloned.1.call-start = ((), (), s32[]{:S(2)}) async-start(), calls=%async_computation.42 | async-start | bytes 9437184 | tf_op jit(solution)/shard_map/all_gather | solution.py:129
  1036.1 623.1 %all-gather.54.cloned.1.call-start = ((), (), s32[]{:S(2)}) async-start(), calls=%async_computation.35 | async-start | bytes 9437184 | tf_op jit(solution)/shard_map/all_gather | solution.py:129
  1036.8 656.3 %reduce-scatter.47.cloned.1.call-start = ((), (), s32[]{:S(2)}) async-start(), calls=%async_computation.48 | async-start | bytes 3145728 | tf_op jit(solution)/shard_map/reduce_scatter | solution.py:144
  1225.7 501.6 %reduce-scatter.45.cloned.1.call-start = ((), (), s32[]{:S(2)}) async-start(), calls=%async_computation.47 | async-start | bytes 3145728 | tf_op jit(solution)/shard_map/reduce_scatter | solution.py:144
  1437.4 391.4 %reduce-scatter.59.cloned.1.call-start = ((), (), s32[]{:S(2)}) async-start(), calls=%async_computation.54 | async-start | bytes 12582912 | tf_op jit(solution)/shard_map/reduce_scatter | solution.py:150
  1447.2 483.0 %reduce-scatter.57.cloned.1.call-start = ((), (), s32[]{:S(2)}) async-start(), calls=%async_computation.53 | async-start | bytes 12582912 | tf_op jit(solution)/shard_map/reduce_scatter | solution.py:150
  1457.2 552.5 %reduce-scatter.43.cloned.1.call-start = ((), (), s32[]{:S(2)}) async-start(), calls=%async_computation.46 | async-start | bytes 9437184 | tf_op jit(solution)/shard_map/reduce_scatter | solution.py:141
  1554.1 535.1 %reduce-scatter.41.cloned.1.call-start = ((), (), s32[]{:S(2)}) async-start(), calls=%async_computation.45 | async-start | bytes 9437184 | tf_op jit(solution)/shard_map/reduce_scatter | solution.py:141
  1571.0 619.6 %reduce-scatter.53.cloned.1.call-start = ((), (), s32[]{:S(2)}) async-start(), calls=%async_computation.51 | async-start | bytes 12582912 | tf_op jit(solution)/shard_map/reduce_scatter | solution.py:147
  1580.5 711.7 %reduce-scatter.49.cloned.1.call-start = ((), (), s32[]{:S(2)}) async-start(), calls=%async_computation.49 | async-start | bytes 12582912 | tf_op jit(solution)/shard_map/reduce_scatter | solution.py:147
  1590.1 848.9 %reduce-scatter.39.cloned.1.call-start = ((), (), s32[]{:S(2)}) async-start(), calls=%async_computation.44 | async-start | bytes 18874368 | tf_op jit(solution)/shard_map/reduce_scatter | solution.py:138
  1606.9 978.8 %reduce-scatter.37.cloned.1.call-start = ((), (), s32[]{:S(2)}) async-start(), calls=%async_computation.43 | async-start | bytes 18874368 | tf_op jit(solution)/shard_map/reduce_scatter | solution.py:138
  1673.7 1016.8 %reduce-scatter.71.cloned.1.call-start = ((), (), s32[]{:S(2)}) async-start(), calls=%async_computation.60 | async-start | bytes 1114112
  1695.5 1012.0 %reduce-scatter.69.cloned.1.call-start = ((), (), s32[]{:S(2)}) async-start(), calls=%async_computation.59 | async-start | bytes 1114112
  1729.7 1053.0 %reduce-scatter.75.cloned.1.call-start = ((), (), s32[]{:S(2)}) async-start(), calls=%async_computation.62 | async-start | bytes 4456448
  1835.3 1023.3 %reduce-scatter.73.cloned.1.call-start = ((), (), s32[]{:S(2)}) async-start(), calls=%async_computation.61 | async-start | bytes 4456448
  1936.8 990.9 %reduce-scatter.67.cloned.1.call-start = ((), (), s32[]{:S(2)}) async-start(), calls=%async_computation.58 | async-start | bytes 3342336
  2014.4 982.1 %reduce-scatter.65.cloned.1.call-start = ((), (), s32[]{:S(2)}) async-start(), calls=%async_computation.57 | async-start | bytes 3342336
  2093.8 977.8 %reduce-scatter.55.cloned.1.call-start = ((), (), s32[]{:S(2)}) async-start(), calls=%async_computation.52 | async-start | bytes 4456448 | tf_op jit(solution)/shard_map/reduce_scatter | solution.py:164
  2190.6 957.1 %reduce-scatter.51.cloned.1.call-start = ((), (), s32[]{:S(2)}) async-start(), calls=%async_computation.50 | async-start | bytes 4456448 | tf_op jit(solution)/shard_map/reduce_scatter | solution.py:164
  2292.3 943.7 %reduce-scatter.63.cloned.1.call-start = ((), (), s32[]{:S(2)}) async-start(), calls=%async_computation.56 | async-start | bytes 6684672
  2447.7 877.2 %reduce-scatter.61.cloned.1.call-start = ((), (), s32[]{:S(2)}) async-start(), calls=%async_computation.55 | async-start | bytes 6684672
  (129 other events, 3018.5 us)
Sparse Core Ops, SparseCore 0:
  10.9 64.5 all-gather.23
  77.7 44.0 all-gather.27
  123.9 36.7 all-gather.31
  162.7 52.1 all-gather.35
  216.3 150.6 all-gather.25
  368.4 80.3 all-gather.29
  450.4 33.1 all-gather.33
  485.1 103.9 all-gather.37
  590.7 103.9 all-gather.39
  703.1 56.0 all-gather.57
  761.3 59.3 all-gather.43
  822.7 39.2 all-gather.61
  864.2 36.4 all-gather.47
  902.8 49.6 all-gather.65
  954.6 48.4 all-gather.51
  1004.5 105.0 all-gather.55
  1110.9 103.9 all-gather.59
  1216.4 103.9 all-gather.41
  1322.0 104.0 all-gather.45
  1427.4 33.0 all-gather.63
  1462.1 33.1 all-gather.49
  1496.8 80.3 all-gather.67
  1578.8 80.3 all-gather.53
  1661.3 31.8 reduce-scatter.46
  1695.5 31.8 reduce-scatter.44
  1729.5 99.2 reduce-scatter.58
  1831.0 99.2 reduce-scatter.56
  1932.6 77.0 reduce-scatter.42
  2012.1 77.0 reduce-scatter.40
  2091.3 99.2 reduce-scatter.52
  2193.0 99.2 reduce-scatter.48
  2294.6 144.4 reduce-scatter.38
  2441.2 144.4 reduce-scatter.36
  2589.3 57.4 reduce-scatter.70
  2650.8 56.5 reduce-scatter.68
  2711.2 71.4 reduce-scatter.74
  2786.8 71.7 reduce-scatter.72
  2862.4 65.2 reduce-scatter.66
  2931.4 65.0 reduce-scatter.64
  3000.3 71.2 reduce-scatter.54
  3075.9 71.7 reduce-scatter.50
  3151.7 84.3 reduce-scatter.62
  3240.3 84.5 reduce-scatter.60
